TPU v7x, 512 devices: a whole 4x4x16 slice. The times are simulated.
512 devices in a mesh: section: 4 (over x_lo, core), fsdp: 32 (over x_hi, z), tensor: 4 (over y).
Axes of the slice: x: 4 (x_hi: 2, x_lo: 2; x = x_hi * 2 + x_lo), y: 4, z: 16, core: 2. Of those that a mesh axis runs over, the one named last changes fastest.
Arguments:
- entering: bfloat16 [4, 16384, 2048], P('section', 'fsdp', 'tensor'), may hold values from -8 to 8
- w_query: bfloat16 [4, 2048, 4096], P('section', 'fsdp', 'tensor'), may hold values from -0.125 to 0.125
- w_keyval: bfloat16 [4, 2048, 4, 256], P('section', 'fsdp', 'tensor'), may hold values from -0.125 to 0.125
- w_out: bfloat16 [4, 4096, 2048], P('section', 'tensor', 'fsdp'), may hold values from -0.09375 to 0.09375
Outputs:
- leaving: bfloat16 [4, 16384, 2048], P('section', 'fsdp', 'tensor')
All inputs are finite; a program needn't handle non-finite values.
Results may differ from a plain program's by a relative error of at most 0.0055.
Values may be sent and summed in bfloat16 or wider, within the bound.
A program may use at most 64 MiB of HBM per device.

v0:
```python
import math
import jax
import jax.numpy as jnp
from jax import lax
from jax.sharding import PartitionSpec as P

HEAD_DIM = 128
EPSILON = 1e-06
ROPE_BASE = 1000000.0
BEFORE_SHARE = 0.6
AFTER_SHARE = 0.4


def shifted(block, axis, distance):
    devices = range(lax.axis_size(axis))
    route = [((i - distance) % len(devices), i) for i in devices]
    return lax.ppermute(block, axis, route)


def rope_tables(length, width):
    half_width = width // 2
    exponent = jnp.arange(half_width, dtype=jnp.float32) * (2.0 / width)
    inverse = jnp.exp(-exponent * math.log(ROPE_BASE))
    angles = jnp.arange(length, dtype=jnp.float32)[:, None] * inverse[None, :]
    return (jnp.cos(angles)[:, None, :], jnp.sin(angles)[:, None, :])


def head_norm_rope(vectors, cosine, sine):
    meansq = jnp.mean(vectors * vectors, axis=-1, keepdims=True)
    normed = vectors * lax.rsqrt(meansq + EPSILON)
    half_width = vectors.shape[-1] // 2
    first_half = normed[..., :half_width]
    second_half = normed[..., half_width:]
    return jnp.concatenate(
        [first_half * cosine - second_half * sine, second_half * cosine + first_half * sine],
        axis=-1,
    )


def pack_weights(query_shard, keyval_shard, out_shard):
    return jnp.concatenate(
        [query_shard.reshape(1, -1), keyval_shard.reshape(1, -1), out_shard.reshape(1, -1)], axis=1
    )


def body(entering, w_query, w_keyval, w_out):
    owned_pack = pack_weights(w_query, w_keyval, w_out)
    from_lower = shifted(owned_pack, "section", 1)
    from_upper = shifted(owned_pack, "section", -1)
    section_pack = (
        BEFORE_SHARE * from_lower.astype(jnp.float32) + AFTER_SHARE * from_upper.astype(jnp.float32)
    ).astype(jnp.bfloat16)
    query_count = w_query.size
    keyval_count = w_keyval.size
    query_mine = section_pack[:, :query_count].reshape(w_query.shape)
    keyval_mine = section_pack[:, query_count : query_count + keyval_count].reshape(w_keyval.shape)
    out_mine = section_pack[:, query_count + keyval_count :].reshape(w_out.shape)
    own_rows = entering[0]
    own_float = own_rows.astype(jnp.float32)
    full_rows = lax.all_gather(own_rows, "tensor", axis=1, tiled=True).astype(jnp.float32)
    meansq = jnp.mean(full_rows * full_rows, axis=-1, keepdims=True)
    normed = (full_rows * lax.rsqrt(meansq + EPSILON)).astype(jnp.bfloat16)
    length = normed.shape[0]
    query_width = query_mine.shape[2]
    keyval_width = keyval_mine.shape[2] * keyval_mine.shape[3]
    query_piece = lax.all_gather(query_mine, "fsdp", axis=1, tiled=True)
    keyval_piece = lax.all_gather(keyval_mine, "fsdp", axis=1, tiled=True)
    piece_rows = query_piece.shape[1]
    query_sum = jnp.dot(normed, query_piece[0], preferred_element_type=jnp.float32)
    keyval_sum = jnp.dot(
        normed, keyval_piece[0].reshape(piece_rows, -1), preferred_element_type=jnp.float32
    )
    query_heads = query_width // HEAD_DIM
    kv_count = keyval_width // (2 * HEAD_DIM)
    group_size = query_heads // kv_count
    cosine, sine = rope_tables(length, HEAD_DIM)
    queries = head_norm_rope(
        query_sum.reshape(length, kv_count, group_size, HEAD_DIM),
        cosine[:, :, None, :],
        sine[:, :, None, :],
    ).astype(jnp.bfloat16)
    keyval_heads = keyval_sum.reshape(length, kv_count, 2 * HEAD_DIM)
    keys = head_norm_rope(keyval_heads[..., :HEAD_DIM], cosine, sine).astype(jnp.bfloat16)
    values = keyval_heads[..., HEAD_DIM:].astype(jnp.bfloat16)
    positions = jnp.arange(length)
    causal = positions[:, None] >= positions[None, :]
    scale = 1.0 / math.sqrt(HEAD_DIM)

    def one_group(query_slice):
        scores = (
            jnp.einsum("qkd,pkd->kqp", query_slice, keys, preferred_element_type=jnp.float32)
            * scale
        )
        expo = jnp.where(causal[None], jnp.exp(scores - math.sqrt(HEAD_DIM)), 0.0)
        weights = (expo / jnp.sum(expo, axis=-1, keepdims=True)).astype(jnp.bfloat16)
        return jnp.einsum(
            "kqp,pkd->qkd", weights, values, preferred_element_type=jnp.float32
        ).astype(jnp.bfloat16)

    mixed = lax.map(one_group, jnp.moveaxis(queries, 2, 0))
    mixed = jnp.moveaxis(mixed, 0, 2).reshape(length, query_heads * HEAD_DIM)
    partial_terms = jnp.dot(
        mixed,
        lax.all_gather(out_mine, "fsdp", axis=2, tiled=True)[0],
        preferred_element_type=jnp.float32,
    ).astype(jnp.bfloat16)
    summed = lax.psum_scatter(partial_terms, "tensor", scatter_dimension=1, tiled=True).astype(
        jnp.float32
    )
    return (own_float + summed).astype(jnp.bfloat16)[None]


def solution(mesh):
    in_specs = (
        P("section", "fsdp", "tensor"),
        P("section", "fsdp", "tensor"),
        P("section", "fsdp", "tensor", None),
        P("section", "tensor", "fsdp"),
    )
    out_specs = P("section", "fsdp", "tensor")
    return jax.shard_map(body, mesh=mesh, in_specs=in_specs, out_specs=out_specs, check_vma=False)
```

profile of v0, /device:TPU:1, one launch (start us, length us, event | category | flops | bytes accessed | tf_op | source)
XLA Modules:
  0.0 575.0 jit_solution(11576316620218176375)
XLA Ops:
  6.5 1.1 copy.29
  7.9 0.8 copy.30
  8.7 1.1 copy.20
  10.4 4.5 collective-permute-start
  14.9 6.2 %collective-permute-start.1 = (bf16[1,147456]{1,0:T(2,128)(2,1)S(1)}, bf16[1,147456]{1,0:T(2,128)(2,1)S(1)}, u32[]{:S(2)}, u32[]{:S(2)}) collective-permute-start(bf16[1,147456]{1,0:T(2,128)(2,1)S(1)} %constant_dynamic-update-slice_fusion.1), channel_id=1, source_target_pairs={{128,0},{256,128},{384,256},{0,384},{129,1},{257,129},{385,257},{1... | collective-permute-start | bytes 884744 | tf_op jit(solution)/shard_map/ppermute | solution.py:17
  21.7 9.4 %collective-permute-done.1 = bf16[1,147456]{1,0:T(2,128)(2,1)S(1)} collective-permute-done((bf16[1,147456]{1,0:T(2,128)(2,1)S(1)}, bf16[1,147456]{1,0:T(2,128)(2,1)S(1)}, u32[]{:S(2)}, u32[]{:S(2)}) %collective-permute-start.1) | collective-permute-done | bytes 294944 | tf_op jit(solution)/shard_map/ppermute | solution.py:17
  31.0 1.4 add_convert_fusion.1
  33.4 1.5 slice_reduce_fusion
  34.9 0.7 reshape.281
  35.7 1.0 fusion.29
  36.8 0.8 copy.26
  37.8 21.9 %all-gather.12.cloned.1.call-done = bf16[1,512,2048]{2,1,0:T(8,128)(2,1)} async-done(((bf16[1,512,512]{2,1,0:T(8,128)(2,1)}), bf16[1,512,2048]{2,1,0:T(8,128)(2,1)}) %all-gather.12.cloned.1.call-update) | async-done | bytes 2097168 | tf_op jit(solution)/shard_map/all_gather | solution.py:60
  59.7 2.2 fusion.11
  62.0 135.2 %all-gather.8.cloned.1.call-done = bf16[1,2048,1,256]{3,1,2,0:T(8,128)(2,1)} async-done(((bf16[1,64,1,256]{3,1,2,0:T(8,128)(2,1)}), bf16[1,2048,1,256]{3,1,2,0:T(8,128)(2,1)}) %all-gather.8.cloned.1.call-update) | async-done | bytes 1048592 | tf_op jit(solution)/shard_map/all_gather | solution.py:67
  197.2 2.1 convolution_bitcast_fusion
  200.2 157.7 %all-gather.6.cloned.1.call-done = bf16[1,2048,1024]{2,1,0:T(8,128)(2,1)} async-done(((bf16[1,64,1024]{2,1,0:T(8,128)(2,1)}), bf16[1,2048,1024]{2,1,0:T(8,128)(2,1)}) %all-gather.6.cloned.1.call-update) | async-done | bytes 4194320 | tf_op jit(solution)/shard_map/all_gather | solution.py:66
  358.0 4.6 fusion.20
  364.4 0.8 subtract_convert_fusion
  365.7 0.6 copy-done.2
  366.4 6.8 %while.13 = (s32[]{:T(128)}, bf16[8,512,1,128]{1,3,0,2:T(8,128)(2,1)S(1)}, bf16[8,512,1,128]{3,1,2,0:T(8,128)(2,1)S(1)}, bf16[512,1,128]{2,0,1:T(8,128)(2,1)S(1)}, bf16[512,1,128]{2,0,1:T(8,128)(2,1)S(1)}, /*index=5*/s32[]{:T(128)}) while((s32[]{:T(128)}, bf16[8,512,1,128]{1,3,0,2:T(8,128)(2,1)S(1)}, ...), condition=%wide.region_5.6_spmd.clone, body=%wide.region_3.5_spmd.clone.sunk | while | flops 136117760 | bytes 3149901 | solution.py:100
  373.2 146.0 %all-gather.10.cloned.1.call-done = bf16[1,1024,2048]{1,2,0:T(8,128)(2,1)} async-done(((bf16[1,1024,64]{1,2,0:T(8,128)(2,1)}), bf16[1,1024,2048]{1,2,0:T(8,128)(2,1)}) %all-gather.10.cloned.1.call-update) | async-done | bytes 4194320 | tf_op jit(solution)/shard_map/all_gather | solution.py:104
  519.1 5.9 %fusion.17 = bf16[512,2048]{1,0:T(8,128)(2,1)} fusion(bf16[512,1024]{0,1:T(8,128)(2,1)S(1)} %bitcast.78, bf16[1,1024,2048]{1,2,0:T(8,128)(2,1)} %all-gather.10.cloned.1.call-done), kind=kOutput, calls=%fused_computation.23 | convolution fusion | flops 2148532224 | bytes 7340032 | tf_op jit(solution)/shard_map/dot_general | solution.py:102
  525.0 41.4 %reduce-scatter.2.cloned.1.call-done = bf16[512,512]{1,0:T(8,128)(2,1)} async-done(((bf16[512,2048]{1,0:T(8,128)(2,1)}), bf16[512,512]{1,0:T(8,128)(2,1)}) %reduce-scatter.2.cloned.1.call-update) | async-done | bytes 524304 | tf_op jit(solution)/shard_map/reduce_scatter | solution.py:107
  566.5 2.0 fusion.27
  (72 shorter events, 12.6 us)
Async XLA Ops:
  6.5 53.2 %all-gather.12.cloned.1.call-start = ((), (), s32[]{:S(2)}) async-start(), calls=%async_computation.5 | async-start | bytes 2621440 | tf_op jit(solution)/shard_map/all_gather | solution.py:60
  10.4 11.3 %collective-permute-start = (bf16[1,147456]{1,0:T(2,128)(2,1)S(1)}, bf16[1,147456]{1,0:T(2,128)(2,1)S(1)}, u32[]{:S(2)}, u32[]{:S(2)}) collective-permute-start(bf16[1,147456]{1,0:T(2,128)(2,1)S(1)} %constant_dynamic-update-slice_fusion.1), channel_id=1, source_target_pairs={{384,0},{0,128},{128,256},{256,384},{385,1},{1,129},{129,257},{257... | collective-permute-start | bytes 884744 | tf_op jit(solution)/shard_map/ppermute | solution.py:17
  14.9 16.2 %collective-permute-start.1 = (bf16[1,147456]{1,0:T(2,128)(2,1)S(1)}, bf16[1,147456]{1,0:T(2,128)(2,1)S(1)}, u32[]{:S(2)}, u32[]{:S(2)}) collective-permute-start(bf16[1,147456]{1,0:T(2,128)(2,1)S(1)} %constant_dynamic-update-slice_fusion.1), channel_id=1, source_target_pairs={{128,0},{256,128},{384,256},{0,384},{129,1},{257,129},{385,257},{1... | collective-permute-start | bytes 884744 | tf_op jit(solution)/shard_map/ppermute | solution.py:17
  21.1 176.1 %all-gather.8.cloned.1.call-start = ((), (), s32[]{:S(2)}) async-start(), calls=%async_computation.2 | async-start | bytes 1081344 | tf_op jit(solution)/shard_map/all_gather | solution.py:67
  33.3 324.6 %all-gather.6.cloned.1.call-start = ((), (), s32[]{:S(2)}) async-start(), calls=%async_computation.1 | async-start | bytes 4325376 | tf_op jit(solution)/shard_map/all_gather | solution.py:66
  35.6 483.5 %all-gather.10.cloned.1.call-start = ((), (), s32[]{:S(2)}) async-start(), calls=%async_computation.3 | async-start | bytes 4325376 | tf_op jit(solution)/shard_map/all_gather | solution.py:104
  37.6 528.8 %reduce-scatter.2.cloned.1.call-start = ((), (), s32[]{:S(2)}) async-start(), calls=%async_computation.4 | async-start | bytes 2621440 | tf_op jit(solution)/shard_map/reduce_scatter | solution.py:107
  59.7 137.5 %copy-start.1 = (bf16[1,512,2048]{2,1,0:T(8,128)(2,1)S(1)}, bf16[1,512,2048]{2,1,0:T(8,128)(2,1)}, u32[]{:S(2)}) copy-start(bf16[1,512,2048]{2,1,0:T(8,128)(2,1)} %all-gather.12.cloned.1.call-done) | copy-start | bytes 6291460
  365.1 1.2 copy-start.2
  525.0 41.4 %copy-start = (bf16[1,512,512]{2,1,0:T(8,128)(2,1)S(1)}, bf16[1,512,512]{2,1,0:T(8,128)(2,1)}, u32[]{:S(2)}) copy-start(bf16[1,512,512]{2,1,0:T(8,128)(2,1)} %param.6) | copy-start | bytes 1572868
Sparse Core Ops, SparseCore 0:
  21.2 38.4 all-gather.11
  62.8 134.3 all-gather.7
  200.3 157.6 all-gather.5
  360.9 158.1 all-gather.9
  525.2 41.2 reduce-scatter.1
where the time goes:
time: 575 us
  waiting for transfers between devices  512 us (89%)
  matrix products  18 us (3%)
  between operations  13.4 us (2%)
  starting transfers between devices  11 us (2%)
  local copies, waits for them, and re-layouts  10.2 us (2%)
  other arithmetic  9.86 us (2%)
    all_gather x1, waiting for transfers between devices, body(): query_piece = lax.all_gather(query_mine, 'fsdp', axis=1, tiled=True)  158 us
    all_gather x1, waiting for transfers between devices, body(): lax.all_gather(out_mine, 'fsdp', axis=2, tiled=True)[0]  146 us
    all_gather x1, waiting for transfers between devices, body(): keyval_piece = lax.all_gather(keyval_mine, 'fsdp', axis=1, tiled=True)  135 us
    reduce_scatter x1, waiting for transfers between devices, body(): lax.psum_scatter(partial_terms, 'tensor', scatter_dimension=1, tiled=True)  41.4 us
    all_gather x1, waiting for transfers between devices, body(): lax.all_gather(own_rows, 'tensor', axis=1, tiled=True).astype(jnp.float32)  21.9 us
  transfers between devices with their start and end apart: 7, of which 7 were waited for; matrix products, arithmetic and copies ran while one was open for 4% of the time, Pallas kernels for 0%

commit v1 on v0

--- a/solution.py
+++ b/solution.py
@@ -9,6 +9,13 @@
 ROPE_BASE = 1000000.0
 BEFORE_SHARE = 0.6
 AFTER_SHARE = 0.4
+
+
+def exchange_gather(shard, axis, along):
+    size = lax.axis_size(axis)
+    blocks = jnp.stack([shard for _ in range(size)])
+    blocks = lax.all_to_all(blocks, axis, split_axis=0, concat_axis=0)
+    return jnp.concatenate(blocks, axis=along)
 
 
 def shifted(block, axis, distance):
@@ -64,7 +71,7 @@
     query_width = query_mine.shape[2]
     keyval_width = keyval_mine.shape[2] * keyval_mine.shape[3]
     query_piece = lax.all_gather(query_mine, "fsdp", axis=1, tiled=True)
-    keyval_piece = lax.all_gather(keyval_mine, "fsdp", axis=1, tiled=True)
+    keyval_piece = exchange_gather(keyval_mine, "fsdp", 1)
     piece_rows = query_piece.shape[1]
     query_sum = jnp.dot(normed, query_piece[0], preferred_element_type=jnp.float32)
     keyval_sum = jnp.dot(

time: 575 us -> 442 us (0.77)
  waiting for transfers between devices: 512 us -> 363 us
  starting transfers between devices: 11 us -> 26.3 us
    all_gather x1 -> x0, waiting for transfers between devices: 135 us -> none  [body(): keyval_piece = lax.all_gather(keyval_mine, 'fsdp', axis=1, tiled=True)]
    all_to_all x0 -> x1, waiting for transfers between devices: none -> 45 us  [exchange_gather(): blocks = lax.all_to_all(blocks, axis, split_axis=0, concat_axis=0)]
    all_gather x1, waiting for transfers between devices: 158 us -> 115 us  [body(): query_piece = lax.all_gather(query_mine, 'fsdp', axis=1, tiled=True)]
    all_gather x1, waiting for transfers between devices: 21.9 us -> 5.44 us  [body(): lax.all_gather(own_rows, 'tensor', axis=1, tiled=True).astype(jnp.float32)]
    all_to_all x0 -> x1, starting transfers between devices: none -> 15.3 us  [exchange_gather(): blocks = lax.all_to_all(blocks, axis, split_axis=0, concat_axis=0)]
  transfers between devices with their start and end apart: 7 -> 7, of which waited for: 7 -> 7; matrix products, arithmetic and copies ran while one was open for 4% -> 6% of each run, Pallas kernels for 0% -> 0%
where the time goes in v1:
time: 442 us
  waiting for transfers between devices  363 us (82%)
  starting transfers between devices  26.3 us (6%)
  matrix products  16.9 us (4%)
  between operations  13.4 us (3%)
  local copies, waits for them, and re-layouts  11.7 us (3%)
  other arithmetic  10.6 us (2%)
    all_gather x1, waiting for transfers between devices, body(): lax.all_gather(out_mine, 'fsdp', axis=2, tiled=True)[0]  146 us
    all_gather x1, waiting for transfers between devices, body(): query_piece = lax.all_gather(query_mine, 'fsdp', axis=1, tiled=True)  115 us
    all_to_all x1, waiting for transfers between devices, exchange_gather(): blocks = lax.all_to_all(blocks, axis, split_axis=0, concat_axis=0)  45 us
    reduce_scatter x1, waiting for transfers between devices, body(): lax.psum_scatter(partial_terms, 'tensor', scatter_dimension=1, tiled=True)  41.4 us
    all_to_all x1, starting transfers between devices, exchange_gather(): blocks = lax.all_to_all(blocks, axis, split_axis=0, concat_axis=0)  15.3 us
    ppermute x2, starting transfers between devices, shifted(): return lax.ppermute(block, axis, route)  10.7 us
    ppermute x2, waiting for transfers between devices, shifted(): return lax.ppermute(block, axis, route)  9.92 us
  transfers between devices with their start and end apart: 7, of which 7 were waited for; matrix products, arithmetic and copies ran while one was open for 6% of the time, Pallas kernels for 0%

profile of v1, /device:TPU:1, one launch (start us, length us, event | category | flops | bytes accessed | tf_op | source)
XLA Modules:
  0.0 442.0 jit_solution(9930856259666038818)
XLA Ops:
  6.5 1.1 copy.29
  7.9 0.8 copy.30
  8.7 1.1 copy.20
  10.4 4.5 %collective-permute-start = (bf16[1,147456]{1,0:T(2,128)(2,1)S(1)}, bf16[1,147456]{1,0:T(2,128)(2,1)S(1)}, u32[]{:S(2)}, u32[]{:S(2)}) collective-permute-start(bf16[1,147456]{1,0:T(2,128)(2,1)S(1)} %constant_dynamic-update-slice_fusion.1), channel_id=1, source_target_pairs={{384,0},{0,128},{128,256},{256,384},{385,1},{1,129},{129,257},{257... | collective-permute-start | bytes 884744 | tf_op jit(solution)/shard_map/ppermute | solution.py:24
  14.9 6.2 %collective-permute-start.1 = (bf16[1,147456]{1,0:T(2,128)(2,1)S(1)}, bf16[1,147456]{1,0:T(2,128)(2,1)S(1)}, u32[]{:S(2)}, u32[]{:S(2)}) collective-permute-start(bf16[1,147456]{1,0:T(2,128)(2,1)S(1)} %constant_dynamic-update-slice_fusion.1), channel_id=1, source_target_pairs={{128,0},{256,128},{384,256},{0,384},{129,1},{257,129},{385,257},{1... | collective-permute-start | bytes 884744 | tf_op jit(solution)/shard_map/ppermute | solution.py:24
  21.7 9.4 %collective-permute-done.1 = bf16[1,147456]{1,0:T(2,128)(2,1)S(1)} collective-permute-done((bf16[1,147456]{1,0:T(2,128)(2,1)S(1)}, bf16[1,147456]{1,0:T(2,128)(2,1)S(1)}, u32[]{:S(2)}, u32[]{:S(2)}) %collective-permute-start.1) | collective-permute-done | bytes 294944 | tf_op jit(solution)/shard_map/ppermute | solution.py:24
  31.0 1.4 add_convert_fusion.1
  32.5 1.5 slice_reduce_fusion
  34.9 1.1 stack.3
  36.0 15.3 %all-to-all-start = ((bf16[32,1,64,1,256]{4,2,3,1,0:T(8,128)(2,1)}), bf16[32,1,64,1,256]{4,2,3,1,0:T(8,128)(2,1)S(1)}, u32[]{:S(2)}, u32[]{:S(2)}) async-start(bf16[32,1,64,1,256]{4,2,3,1,0:T(8,128)(2,1)} %stack.3), calls=%async_computation | async-start | bytes 2097152 | tf_op jit(solution)/shard_map/all_to_all | solution.py:17
  51.4 1.7 fusion.28
  53.2 0.8 copy.26
  54.3 5.4 %all-gather.9.cloned.1.call-done = bf16[1,512,2048]{2,1,0:T(8,128)(2,1)} async-done(((bf16[1,512,512]{2,1,0:T(8,128)(2,1)}), bf16[1,512,2048]{2,1,0:T(8,128)(2,1)}) %all-gather.9.cloned.1.call-update) | async-done | bytes 2097168 | tf_op jit(solution)/shard_map/all_gather | solution.py:67
  59.7 2.2 fusion.11
  62.0 45.0 %all-to-all-done = bf16[32,1,64,1,256]{4,2,3,1,0:T(8,128)(2,1)S(1)} async-done(((bf16[32,1,64,1,256]{4,2,3,1,0:T(8,128)(2,1)}), bf16[32,1,64,1,256]{4,2,3,1,0:T(8,128)(2,1)S(1)}, u32[]{:S(2)}, u32[]{:S(2)}) %all-to-all-start) | async-done | bytes 1048608 | tf_op jit(solution)/shard_map/all_to_all | solution.py:17
  106.9 0.9 convolution_bitcast_fusion
  109.4 115.4 %all-gather.5.cloned.1.call-done = bf16[1,2048,1024]{2,1,0:T(8,128)(2,1)} async-done(((bf16[1,64,1024]{2,1,0:T(8,128)(2,1)}), bf16[1,2048,1024]{2,1,0:T(8,128)(2,1)}) %all-gather.5.cloned.1.call-update) | async-done | bytes 4194320 | tf_op jit(solution)/shard_map/all_gather | solution.py:73
  224.8 4.6 %fusion.20 = f32[64,8,8,128]{3,1,2,0:T(8,128)S(1)} fusion(bf16[1,2048,1024]{2,1,0:T(8,128)(2,1)} %all-gather.5.cloned.1.call-done, bf16[1,512,2048]{2,1,0:T(8,128)(2,1)S(1)} %copy-done.1, f32[512]{0:T(512)S(1)} %add_rsqrt_fusion.2), kind=kOutput, calls=%fused_computation.28 | convolution fusion | flops 2150629376 | bytes 8390656 | tf_op jit(solution)/shard_map/dot_general | solution.py:76
  231.6 0.8 subtract_convert_fusion
  233.7 6.8 %while.13 = (s32[]{:T(128)}, bf16[8,512,1,128]{1,3,0,2:T(8,128)(2,1)S(1)}, bf16[8,512,1,128]{3,1,2,0:T(8,128)(2,1)S(1)}, bf16[512,1,128]{2,0,1:T(8,128)(2,1)S(1)}, bf16[512,1,128]{2,0,1:T(8,128)(2,1)S(1)}, /*index=5*/s32[]{:T(128)}) while((s32[]{:T(128)}, bf16[8,512,1,128]{1,3,0,2:T(8,128)(2,1)S(1)}, ...), condition=%wide.region_5.6_spmd.clone, body=%wide.region_3.5_spmd.clone.sunk | while | flops 136117760 | bytes 3149901 | solution.py:107
  240.5 145.7 %all-gather.7.cloned.1.call-done = bf16[1,1024,2048]{1,2,0:T(8,128)(2,1)} async-done(((bf16[1,1024,64]{1,2,0:T(8,128)(2,1)}), bf16[1,1024,2048]{1,2,0:T(8,128)(2,1)}) %all-gather.7.cloned.1.call-update) | async-done | bytes 4194320 | tf_op jit(solution)/shard_map/all_gather | solution.py:111
  386.1 5.9 %fusion.17 = bf16[512,2048]{1,0:T(8,128)(2,1)} fusion(bf16[512,1024]{0,1:T(8,128)(2,1)S(1)} %bitcast.78, bf16[1,1024,2048]{1,2,0:T(8,128)(2,1)} %all-gather.7.cloned.1.call-done), kind=kOutput, calls=%fused_computation.23 | convolution fusion | flops 2148532224 | bytes 7340032 | tf_op jit(solution)/shard_map/dot_general | solution.py:109
  392.0 41.4 %reduce-scatter.2.cloned.1.call-done = bf16[512,512]{1,0:T(8,128)(2,1)} async-done(((bf16[512,2048]{1,0:T(8,128)(2,1)}), bf16[512,512]{1,0:T(8,128)(2,1)}) %reduce-scatter.2.cloned.1.call-update) | async-done | bytes 524304 | tf_op jit(solution)/shard_map/reduce_scatter | solution.py:114
  433.5 2.0 fusion.26
  (76 shorter events, 14.3 us)
Async XLA Ops:
  6.5 53.2 %all-gather.9.cloned.1.call-start = ((), (), s32[]{:S(2)}) async-start(), calls=%async_computation.5 | async-start | bytes 2621440 | tf_op jit(solution)/shard_map/all_gather | solution.py:67
  10.4 11.3 %collective-permute-start = (bf16[1,147456]{1,0:T(2,128)(2,1)S(1)}, bf16[1,147456]{1,0:T(2,128)(2,1)S(1)}, u32[]{:S(2)}, u32[]{:S(2)}) collective-permute-start(bf16[1,147456]{1,0:T(2,128)(2,1)S(1)} %constant_dynamic-update-slice_fusion.1), channel_id=1, source_target_pairs={{384,0},{0,128},{128,256},{256,384},{385,1},{1,129},{129,257},{257... | collective-permute-start | bytes 884744 | tf_op jit(solution)/shard_map/ppermute | solution.py:24
  14.9 16.2 %collective-permute-start.1 = (bf16[1,147456]{1,0:T(2,128)(2,1)S(1)}, bf16[1,147456]{1,0:T(2,128)(2,1)S(1)}, u32[]{:S(2)}, u32[]{:S(2)}) collective-permute-start(bf16[1,147456]{1,0:T(2,128)(2,1)S(1)} %constant_dynamic-update-slice_fusion.1), channel_id=1, source_target_pairs={{128,0},{256,128},{384,256},{0,384},{129,1},{257,129},{385,257},{1... | collective-permute-start | bytes 884744 | tf_op jit(solution)/shard_map/ppermute | solution.py:24
  21.1 203.8 %all-gather.5.cloned.1.call-start = ((), (), s32[]{:S(2)}) async-start(), calls=%async_computation.2 | async-start | bytes 4325376 | tf_op jit(solution)/shard_map/all_gather | solution.py:73
  36.0 70.9 %all-to-all-start = ((bf16[32,1,64,1,256]{4,2,3,1,0:T(8,128)(2,1)}), bf16[32,1,64,1,256]{4,2,3,1,0:T(8,128)(2,1)S(1)}, u32[]{:S(2)}, u32[]{:S(2)}) async-start(bf16[32,1,64,1,256]{4,2,3,1,0:T(8,128)(2,1)} %stack.3), calls=%async_computation | async-start | bytes 2097152 | tf_op jit(solution)/shard_map/all_to_all | solution.py:17
  51.3 334.8 %all-gather.7.cloned.1.call-start = ((), (), s32[]{:S(2)}) async-start(), calls=%async_computation.3 | async-start | bytes 4325376 | tf_op jit(solution)/shard_map/all_gather | solution.py:111
  54.0 379.4 %reduce-scatter.2.cloned.1.call-start = ((), (), s32[]{:S(2)}) async-start(), calls=%async_computation.4 | async-start | bytes 2621440 | tf_op jit(solution)/shard_map/reduce_scatter | solution.py:114
  59.7 47.2 %copy-start.1 = (bf16[1,512,2048]{2,1,0:T(8,128)(2,1)S(1)}, bf16[1,512,2048]{2,1,0:T(8,128)(2,1)}, u32[]{:S(2)}) copy-start(bf16[1,512,2048]{2,1,0:T(8,128)(2,1)} %all-gather.9.cloned.1.call-done) | copy-start | bytes 6291460
  230.7 1.0 copy-start.2
  232.4 0.9 copy-start.3
  232.4 1.3 copy-start.4
  392.0 41.4 %copy-start = (bf16[1,512,512]{2,1,0:T(8,128)(2,1)S(1)}, bf16[1,512,512]{2,1,0:T(8,128)(2,1)}, u32[]{:S(2)}) copy-start(bf16[1,512,512]{2,1,0:T(8,128)(2,1)} %param.6) | copy-start | bytes 1572868
Sparse Core Ops, SparseCore 0:
  21.2 38.4 all-gather.8
  62.8 161.9 all-gather.4
  228.0 158.1 all-gather.6
  392.2 41.2 reduce-scatter.1
